TPU v7x, 128 devices: a whole 4x4x4 slice. The times are simulated.
128 devices in a mesh: prow: 8 (over y_lo, z), pcol: 16 (over x, y_hi, core).
Axes of the slice: x: 4, y: 4 (y_hi: 2, y_lo: 2; y = y_hi * 2 + y_lo), z: 4, core: 2. Of those that a mesh axis runs over, the one named last changes fastest.
Arguments:
- anc_inverse: float32 [4096, 4096], P('pcol', 'prow')
- pattern_one: int32 [16, 8], replicated, may hold values from 0 to 15, as said below
- parents: int32 [16], replicated, may hold values from 0 to 15, as said below
- low_one: float32 [16, 2048, 256], P('pcol', 'prow'), may hold values from -2 to 2
- pivot_one: float32 [16, 256, 256], P('pcol'), may hold values from -4 to 4
- low_two: float32 [16, 2048, 256], P('pcol', 'prow'), may hold values from -2 to 2
- second_scaled_factor: float32 [16, 256, 256], P('pcol'), may hold values from -2 to 2
- second_pivot_inverse: float32 [16, 256, 256], P('pcol'), may hold values from -4 to 4
Outputs:
- column_one: float32 [16, 4096, 256], P('prow', 'pcol')
- diag_one: float32 [16, 256, 256], P('pcol')
- column_two: float32 [16, 4096, 256], P('prow', 'pcol')
- second_parent_inverse: float32 [16, 256, 256], P('pcol')
- second_diagonal_inverse: float32 [16, 256, 256], P('pcol')
Inputs may be any that keep to these rules, and one draw needn't show every extreme that they name: `pattern_one`: entry r of each row names an ancestor of process row r: it lies in r * 2 to r * 2 + 1; for each r, every ancestor of that range is entry r of exactly 8 rows. `parents`: every first-level supernode is the parent of exactly one second-level supernode.
All inputs are finite; a program needn't handle non-finite values.
Results may differ from a plain program's by a relative error of at most 0.000073.
Values sent between devices are 32-bit elements; how exact they have to be, the bound alone decides.
No kernel may reach another device: no remote copies, remote signals or barrier semaphores. Data moves between devices by JAX's collectives and lax.ppermute only.
A program may use at most 128 MiB of HBM per device.

v0:
```python
import jax
import jax.numpy as jnp
from jax import lax
from jax.sharding import PartitionSpec as P


def in_one_piece(arrays, axis, dim, along):
    widths = [a.shape[along] for a in arrays]
    both = jnp.concatenate(arrays, axis=along)
    result = lax.all_gather(both, axis, axis=dim, tiled=True)
    return tuple(jnp.split(result, [sum(widths[:k]) for k in range(1, len(widths))], axis=along))


def sent_to_all(x, axis):
    copies = jnp.broadcast_to(x, (lax.axis_size(axis), *x.shape))
    return lax.all_to_all(copies, axis, split_axis=0, concat_axis=0, tiled=True)


def over_copies(x, axis):
    return sent_to_all(x, axis).sum(axis=0)


def side_by_side(arrays, axis, dim, along):
    both = jnp.concatenate(arrays, axis=along)
    result, at, outs = (lax.psum_scatter(both, axis, scatter_dimension=dim, tiled=True), 0, [])
    for a in arrays:
        outs.append(lax.slice_in_dim(result, at, at + a.shape[along], axis=along))
        at += a.shape[along]
    return tuple(outs)


def together(arrays, axis):
    line, at, outs = (jnp.concatenate([a.reshape(-1) for a in arrays]), 0, [])
    subtotal = over_copies(line, axis)
    for a in arrays:
        outs.append(subtotal[at : at + a.size].reshape(a.shape))
        at += a.size
    return tuple(outs)


def batched(left, right):
    return jnp.einsum("kab,kbd->kad", left, right, precision=lax.Precision.HIGHEST)


def batched_left_t(left, right):
    return jnp.einsum("kba,kbd->kad", left, right, precision=lax.Precision.HIGHEST)


def pick_rows(hit_mask, count):
    total = hit_mask.shape[0]
    keys = jnp.where(hit_mask, 0, total).astype(jnp.int32) + jnp.arange(total, dtype=jnp.int32)
    chosen_rows = jnp.argsort(keys)[:count]
    valid = jnp.take(hit_mask, chosen_rows, axis=0).astype(jnp.float32)[:, None, None]
    return (chosen_rows, valid)


def body(
    anc_inverse,
    pattern_one,
    parents,
    low_one,
    pivot_one,
    low_two,
    second_scaled_factor,
    second_pivot_inverse,
):
    my_row = lax.axis_index("prow")
    my_col = lax.axis_index("pcol")
    row_count = lax.axis_size("prow")
    col_count = lax.axis_size("pcol")
    per_row_anc = col_count // row_count
    supernode_block_width = pivot_one.shape[1]
    per_col_one = pivot_one.shape[0]
    per_col_two = second_scaled_factor.shape[0]
    owned = anc_inverse.shape[1] // supernode_block_width
    zblocks = anc_inverse.reshape(supernode_block_width, owned, supernode_block_width).transpose(
        1, 0, 2
    )
    lowall = lax.all_gather(low_one, "pcol", axis=0, tiled=True)
    total_one = lowall.shape[0]
    owned_slot_list = lax.dynamic_index_in_dim(pattern_one, my_row, 1, keepdims=False)
    chosen = jnp.take(zblocks, owned_slot_list - my_row * owned, axis=0)
    first_terms = batched(chosen, lowall)
    lowsec, topall = in_one_piece((low_two, second_scaled_factor), "pcol", 0, 1)
    total_two = lowsec.shape[0]
    pattern_two = jnp.take(pattern_one, parents, axis=0)
    my_slots_two = lax.dynamic_index_in_dim(pattern_two, my_row, 1, keepdims=False)
    chosen_two = jnp.take(zblocks, my_slots_two - my_row * owned, axis=0)
    first_full = -lax.psum(first_terms, "prow")
    share = total_two // row_count
    start = my_row * share
    parents_share = lax.dynamic_slice_in_dim(parents, start, share, 0)
    tops_share = lax.dynamic_slice_in_dim(topall, start, share, 0)
    carried = batched(jnp.take(first_full, parents_share, axis=0), tops_share)
    base_terms = batched(chosen_two, lowsec)
    updated = lax.dynamic_slice_in_dim(base_terms, start, share, 0) + carried
    second_terms = lax.dynamic_update_slice_in_dim(base_terms, updated, start, 0)
    second_full = -lax.psum(second_terms, "prow")
    rows_one, valid_one = pick_rows(owned_slot_list == my_col, total_one // per_row_anc)
    pivot_small = valid_one * batched_left_t(
        jnp.take(lowall, rows_one, axis=0), jnp.take(first_full, rows_one, axis=0)
    )
    pivot_terms = jnp.zeros_like(first_full).at[rows_one].add(pivot_small)
    pivot_part = lax.psum_scatter(pivot_terms, "pcol", scatter_dimension=0, tiled=True)
    pivot_sum = over_copies(pivot_part, "prow")
    diag_one = pivot_one - pivot_sum
    count_one = first_full.shape[0] // row_count
    column_one = lax.dynamic_slice_in_dim(first_full, my_row * count_one, count_one, 0)
    second_level_count = second_full.shape[0] // row_count
    column_two = lax.dynamic_slice_in_dim(
        second_full, my_row * second_level_count, second_level_count, 0
    )
    rows_two, valid_two = pick_rows(my_slots_two == my_col, total_two // per_row_anc)
    lows_picked = jnp.take(lowsec, rows_two, axis=0)
    parent_picked = jnp.take(first_full, jnp.take(parents, rows_two, axis=0), axis=0)
    cross_small = valid_two * batched_left_t(parent_picked, lows_picked)
    diag_small = valid_two * batched_left_t(lows_picked, jnp.take(second_full, rows_two, axis=0))
    local_parent = parents - my_col * per_col_one
    own_parent = (local_parent >= 0) & (local_parent < per_col_one)
    rows_own, valid_own = pick_rows(own_parent, per_col_two)
    valid_own = valid_own * (my_row == 0).astype(jnp.float32)
    local_picked = jnp.clip(jnp.take(local_parent, rows_own, axis=0), 0, per_col_one - 1)
    picked = jnp.take(diag_one, local_picked, axis=0)
    own_small = valid_own * batched(picked, jnp.take(topall, rows_own, axis=0))
    cross_terms = (
        jnp.zeros_like(second_full).at[rows_two].add(cross_small).at[rows_own].add(own_small)
    )
    diag_terms = jnp.zeros_like(second_full).at[rows_two].add(diag_small)
    part_cross, part_diag = side_by_side((cross_terms, diag_terms), "pcol", 0, 1)
    sum_cross, sum_diag = together((part_cross, part_diag), "prow")
    second_parent_inverse = -sum_cross
    second_diagonal_inverse = (
        second_pivot_inverse
        - batched_left_t(second_scaled_factor, second_parent_inverse)
        - sum_diag
    )
    return (column_one, diag_one, column_two, second_parent_inverse, second_diagonal_inverse)


def solution(mesh):
    placed = (
        P("pcol", "prow"),
        P(),
        P(),
        P("pcol", "prow", None),
        P("pcol", None, None),
        P("pcol", "prow", None),
        P("pcol", None, None),
        P("pcol", None, None),
    )
    return jax.shard_map(
        body,
        mesh=mesh,
        in_specs=placed,
        out_specs=(
            P("prow", "pcol", None),
            P("pcol", None, None),
            P("prow", "pcol", None),
            P("pcol", None, None),
            P("pcol", None, None),
        ),
        check_vma=False,
    )
```

profile of v0, /device:TPU:1, one launch (start us, length us, event | category | flops | bytes accessed | tf_op | source)
XLA Modules:
  0.0 673.7 jit_solution(4868192869001686954)
XLA Ops:
  11.0 2.8 gather_fusion.3
  13.8 56.2 %all-gather.3.cloned.1.call-done = f32[16,256,256]{2,1,0:T(8,128)} async-done(((f32[1,256,256]{2,1,0:T(8,128)}), f32[16,256,256]{2,1,0:T(8,128)}) %all-gather.3.cloned.1.call-update) | async-done | bytes 4194320 | tf_op jit(solution)/shard_map/all_gather | solution.py:79
  70.0 9.7 %fusion.2 = f32[16,256,256]{2,1,0:T(8,128)} fusion(f32[16,256,256]{2,1,0:T(8,128)} %all-gather.3.cloned.1.call-done, f32[16,256,256]{2,1,0:T(8,128)} %gather_fusion.3, pred[16]{0:T(512)(128)(4,1)S(1)} %compare_and_fusion.4), kind=kOutput, calls=%fused_computation.18 | convolution fusion | flops 3222274048 | bytes 12582928 | tf_op jit(solution)/shard_map/kab,kbd->kad/dot_general | solution.py:42
  83.8 4.2 gather_fusion.5
  88.0 95.9 %all-reduce.3.cloned.1.call-done = f32[16,256,256]{2,1,0:T(8,128)} async-done(((f32[16,256,256]{2,1,0:T(8,128)}), f32[16,256,256]{2,1,0:T(8,128)}) %all-reduce.3.cloned.1.call-update) | async-done | bytes 4194320 | tf_op jit(solution)/shard_map/psum | solution.py:89
  183.9 4.5 neg.15
  188.4 4.2 gather_fusion.6
  192.6 6.1 fusion.17
  201.1 4.4 scatter_fusion
  207.0 2.7 gather_fusion.7
  209.8 2.8 gather_fusion.1
  212.6 46.1 %all-gather.5.cloned.1.call-done = f32[16,512,256]{2,1,0:T(8,128)} async-done(((f32[1,512,256]{2,1,0:T(8,128)}), f32[16,512,256]{2,1,0:T(8,128)}) %all-gather.5.cloned.1.call-update) | async-done | bytes 8388624 | tf_op jit(solution)/shard_map/all_gather | solution.py:10
  258.7 6.4 fusion.67
  267.2 5.6 fusion
  275.4 63.5 %reduce-scatter.3.cloned.1.call-done = f32[1,256,256]{2,1,0:T(8,128)} async-done(((f32[16,256,256]{2,1,0:T(8,128)}), f32[1,256,256]{2,1,0:T(8,128)}) %reduce-scatter.3.cloned.1.call-update) | async-done | bytes 262160 | tf_op jit(solution)/shard_map/reduce_scatter | solution.py:104
  341.5 4.4 all-to-all-start
  353.0 4.2 gather_fusion.9
  357.2 2.9 gather_fusion.10
  360.1 6.7 %fusion.22 = f32[8,256,256]{2,1,0:T(8,128)} fusion(f32[8,256,256]{2,1,0:T(8,128)S(1)} %gather_fusion.10, f32[8,256,256]{2,1,0:T(8,128)} %gather_fusion.9, f32[8]{0:T(128)S(1)} %get-tuple-element.106, pred[8]{0:T(512)(128)(4,1)S(1)} %get-tuple-element.93, pred[8]{0:T(512)(128)(4,1)S(1)} %get-tuple-element.91), kind=kOutput, calls=%fused_computation.34 | convolution fusion | flops 1612185600 | bytes 6291504 | tf_op jit(solution)/shard_map/kba,kbd->kad/dot_general | solution.py:46
  369.3 5.3 scatter_fusion.1
  374.6 90.7 %all-reduce.5.cloned.1.call-done = f32[16,256,256]{2,1,0:T(8,128)} async-done(((f32[16,256,256]{2,1,0:T(8,128)}), f32[16,256,256]{2,1,0:T(8,128)}) %all-reduce.5.cloned.1.call-update) | async-done | bytes 4194320 | tf_op jit(solution)/shard_map/psum | solution.py:98
  465.3 4.5 neg.16
  469.7 4.2 gather_fusion.11
  474.0 6.7 fusion.27
  483.0 4.4 scatter_fusion.2
  489.2 2.8 fusion.36
  492.0 7.4 %pad_maximum_fusion = f32[16,512,256]{2,1,0:T(8,128)} fusion(f32[16,256,256]{2,1,0:T(8,128)} %scatter_fusion.2, f32[16,256,256]{2,1,0:T(8,128)} %fusion.36), kind=kLoop, calls=%fused_computation.15 | loop fusion | flops 2097152 | bytes 16777216 | tf_op jit(solution)/shard_map/concatenate | solution.py:24
  499.5 100.2 %reduce-scatter.5.cloned.1.call-done = f32[1,512,256]{2,1,0:T(8,128)} async-done(((f32[16,512,256]{2,1,0:T(8,128)}), f32[1,512,256]{2,1,0:T(8,128)}) %reduce-scatter.5.cloned.1.call-update) | async-done | bytes 524304 | tf_op jit(solution)/shard_map/reduce_scatter | solution.py:25
  601.1 4.1 broadcast_in_dim.125
  605.2 4.9 all-to-all-start.1
  614.0 44.8 %all-to-all-done.1 = f32[8,1,131072]{2,1,0:T(1,128)} async-done(((f32[8,1,131072]{2,1,0:T(1,128)}), f32[8,1,131072]{2,1,0:T(1,128)}, u32[]{:S(2)}, u32[]{:S(2)}) %all-to-all-start.1) | async-done | bytes 4194336 | tf_op jit(solution)/shard_map/all_to_all | solution.py:16
  658.8 5.2 reduce_sum.22
  (96 shorter events, 39.1 us)
Async XLA Ops:
  7.2 62.9 %all-gather.3.cloned.1.call-start = ((), (), s32[]{:S(2)}) async-start(), calls=%async_computation.4 | async-start | bytes 4456448 | tf_op jit(solution)/shard_map/all_gather | solution.py:79
  7.9 176.0 %all-reduce.3.cloned.1.call-start = ((), (), s32[]{:S(2)}) async-start(), calls=%async_computation.5 | async-start | bytes 8388608 | tf_op jit(solution)/shard_map/psum | solution.py:89
  79.7 0.9 copy-start.6
  79.7 1.0 copy-start.9
  79.8 178.9 %all-gather.5.cloned.1.call-start = ((), (), s32[]{:S(2)}) async-start(), calls=%async_computation.7 | async-start | bytes 8912896 | tf_op jit(solution)/shard_map/all_gather | solution.py:10
  81.6 257.4 %reduce-scatter.3.cloned.1.call-start = ((), (), s32[]{:S(2)}) async-start(), calls=%async_computation.6 | async-start | bytes 4456448 | tf_op jit(solution)/shard_map/reduce_scatter | solution.py:104
  201.1 4.9 copy-start
  205.5 259.8 %all-reduce.5.cloned.1.call-start = ((), (), s32[]{:S(2)}) async-start(), calls=%async_computation.8 | async-start | bytes 8388608 | tf_op jit(solution)/shard_map/psum | solution.py:98
  258.7 7.2 %copy-start.1 = (f32[16,512,256]{2,1,0:T(8,128)S(1)}, f32[16,512,256]{2,1,0:T(8,128)}, u32[]{:S(2)}) copy-start(f32[16,512,256]{2,1,0:T(8,128)} %all-gather.5.cloned.1.call-done) | copy-start | bytes 25165828
  258.7 8.5 %copy-start.2 = (f32[16,256,256]{2,1,0:T(8,128)S(1)}, f32[16,256,256]{2,1,0:T(8,128)}, u32[]{:S(2)}) copy-start(f32[16,256,256]{2,1,0:T(8,128)} %gather_fusion.7) | copy-start | bytes 12582916
  267.2 5.6 copy-start.4
  275.4 76.9 %copy-start.10 = (s32[3]{0:T(128)S(1)}, s32[3]{0:T(128)}, u32[]{:S(2)}) copy-start(s32[3]{0:T(128)} %constant.173.clone.1) | copy-start | bytes 40
  341.5 145.9 %all-to-all-start = ((f32[8,1,256,256]{3,2,1,0:T(8,128)}), f32[8,1,256,256]{3,2,1,0:T(8,128)}, u32[]{:S(2)}, u32[]{:S(2)}) async-start(f32[8,1,256,256]{3,2,1,0:T(8,128)} %broadcast_in_dim.110), calls=%async_computation.1 | async-start | bytes 4194304 | tf_op jit(solution)/shard_map/all_to_all | solution.py:16
  345.9 253.8 %reduce-scatter.5.cloned.1.call-start = ((), (), s32[]{:S(2)}) async-start(), calls=%async_computation.9 | async-start | bytes 8912896 | tf_op jit(solution)/shard_map/reduce_scatter | solution.py:25
  480.7 2.4 copy-start.3
  483.0 6.1 copy-start.7
  489.2 10.2 %copy-start.5 = (f32[1,256,256]{2,1,0:T(8,128)}, f32[1,256,256]{2,1,0:T(8,128)S(1)}, u32[]{:S(2)}) copy-start(f32[1,256,256]{2,1,0:T(8,128)S(1)} %bitcast_subtract_fusion) | copy-start | bytes 786436
  605.2 4.9 copy-start.8
  605.2 53.5 %all-to-all-start.1 = ((f32[8,1,131072]{2,1,0:T(1,128)}), f32[8,1,131072]{2,1,0:T(1,128)}, u32[]{:S(2)}, u32[]{:S(2)}) async-start(f32[8,1,131072]{2,1,0:T(1,128)} %broadcast_in_dim.125), calls=%async_computation.3 | async-start | bytes 8388608 | tf_op jit(solution)/shard_map/all_to_all | solution.py:16
Sparse Core Ops, SparseCore 0:
  10.4 59.5 all-gather.2
  79.9 103.9 all-reduce.2
  186.9 71.8 all-gather.4
  262.6 76.3 reduce-scatter.2
  341.5 123.7 all-reduce.4
  499.6 100.0 reduce-scatter.4
where the time goes:
time: 683 us; the launch traced here: 674 us
  waiting for transfers between devices  498 us (73%)
  local copies, waits for them, and re-layouts  64.3 us (9%)
  other arithmetic  44.5 us (7%)
  matrix products  40.7 us (6%)
  between operations  16 us (2%)
  starting transfers between devices  9.97 us (1%)
    reduce_scatter x1, waiting for transfers between devices, side_by_side(): lax.psum_scatter(both, axis, scatter_dimension=dim, tiled=True)  100 us
    psum x1, waiting for transfers between devices, body(): first_full = -lax.psum(first_terms, 'prow')  95.9 us
    psum x1, waiting for transfers between devices, body(): second_full = -lax.psum(second_terms, 'prow')  90.7 us
    reduce_scatter x1, waiting for transfers between devices, body(): lax.psum_scatter(pivot_terms, 'pcol', scatter_dimension=0, tiled=True)  63.5 us
    all_gather x1, waiting for transfers between devices, body(): lowall = lax.all_gather(low_one, 'pcol', axis=0, tiled=True)  56.2 us
    all_gather x1, waiting for transfers between devices, in_one_piece(): result = lax.all_gather(both, axis, axis=dim, tiled=True)  46.1 us
    all_to_all x2, waiting for transfers between devices, sent_to_all(): return lax.all_to_all(copies, axis, split_axis=0, concat_axis=0, tiled=True)  44.8 us
    dot_general x4, matrix products, batched(): jnp.einsum('kab,kbd->kad', left, right, precision=lax.Precision.HIGHEST)  20.6 us
  transfers between devices with their start and end apart: 8, of which 7 were waited for; matrix products, arithmetic and copies ran while one was open for 17% of the time, Pallas kernels for 0%

commit v1 on v0

--- a/solution.py
+++ b/solution.py
@@ -1,7 +1,16 @@
+import functools
 import jax
 import jax.numpy as jnp
 from jax import lax
 from jax.sharding import PartitionSpec as P
+
+
+def part_thing_over_axis(load, ax_name):
+    tmp = jnp.sum(lax.all_gather(load, ax_name), 0)
+    return tmp
+
+
+remake_the_blocks = functools.partial(part_thing_over_axis, ax_name="prow")
 
 
 def in_one_piece(arrays, axis, dim, along):
@@ -95,7 +104,7 @@
     base_terms = batched(chosen_two, lowsec)
     updated = lax.dynamic_slice_in_dim(base_terms, start, share, 0) + carried
     second_terms = lax.dynamic_update_slice_in_dim(base_terms, updated, start, 0)
-    second_full = -lax.psum(second_terms, "prow")
+    second_full = -remake_the_blocks(second_terms)
     rows_one, valid_one = pick_rows(owned_slot_list == my_col, total_one // per_row_anc)
     pivot_small = valid_one * batched_left_t(
         jnp.take(lowall, rows_one, axis=0), jnp.take(first_full, rows_one, axis=0)

time: 683 us -> 916 us (1.34)
  waiting for transfers between devices: 498 us -> 713 us
  other arithmetic: 44.5 us -> 58.8 us
    all_gather x0 -> x1, waiting for transfers between devices: none -> 294 us  [part_thing_over_axis(): tmp = jnp.sum(lax.all_gather(load, ax_name), 0)]
    psum x1 -> x0, waiting for transfers between devices: 90.7 us -> none  [body(): second_full = -lax.psum(second_terms, 'prow')]
    all_to_all x2, waiting for transfers between devices: 44.8 us -> 60.1 us  [sent_to_all(): return lax.all_to_all(copies, axis, split_axis=0, concat_axis=0, tiled=True)]
    reduce_sum x0 -> x1, other arithmetic: none -> 14.3 us  [part_thing_over_axis(): tmp = jnp.sum(lax.all_gather(load, ax_name), 0)]
  transfers between devices with their start and end apart: 8 -> 8, of which waited for: 7 -> 8; matrix products, arithmetic and copies ran while one was open for 17% -> 10% of each run, Pallas kernels for 0% -> 0%
where the time goes in v1:
time: 916 us; the launch traced here: 906 us
  waiting for transfers between devices  713 us (78%)
  local copies, waits for them, and re-layouts  65.8 us (7%)
  other arithmetic  58.8 us (6%)
  matrix products  42.4 us (5%)
  between operations  16 us (2%)
  starting transfers between devices  9.93 us (1%)
    all_gather x1, waiting for transfers between devices, part_thing_over_axis(): tmp = jnp.sum(lax.all_gather(load, ax_name), 0)  294 us
    reduce_scatter x1, waiting for transfers between devices, side_by_side(): lax.psum_scatter(both, axis, scatter_dimension=dim, tiled=True)  99.5 us
    psum x1, waiting for transfers between devices, body(): first_full = -lax.psum(first_terms, 'prow')  95.9 us
    reduce_scatter x1, waiting for transfers between devices, body(): lax.psum_scatter(pivot_terms, 'pcol', scatter_dimension=0, tiled=True)  60.6 us
    all_to_all x2, waiting for transfers between devices, sent_to_all(): return lax.all_to_all(copies, axis, split_axis=0, concat_axis=0, tiled=True)  60.1 us
    all_gather x1, waiting for transfers between devices, body(): lowall = lax.all_gather(low_one, 'pcol', axis=0, tiled=True)  56.2 us
    all_gather x1, waiting for transfers between devices, in_one_piece(): result = lax.all_gather(both, axis, axis=dim, tiled=True)  45.9 us
    dot_general x4, matrix products, batched(): jnp.einsum('kab,kbd->kad', left, right, precision=lax.Precision.HIGHEST)  22.3 us
  transfers between devices with their start and end apart: 8, of which 8 were waited for; matrix products, arithmetic and copies ran while one was open for 10% of the time, Pallas kernels for 0%

profile of v1, /device:TPU:1, one launch (start us, length us, event | category | flops | bytes accessed | tf_op | source)
XLA Modules:
  0.0 906.3 jit_solution(16188759240108930172)
XLA Ops:
  11.0 2.8 gather_fusion.3
  13.8 56.2 %all-gather.4.cloned.1.call-done = f32[16,256,256]{2,1,0:T(8,128)} async-done(((f32[1,256,256]{2,1,0:T(8,128)}), f32[16,256,256]{2,1,0:T(8,128)}) %all-gather.4.cloned.1.call-update) | async-done | bytes 4194320 | tf_op jit(solution)/shard_map/all_gather | solution.py:88
  70.0 9.7 %fusion.2 = f32[16,256,256]{2,1,0:T(8,128)} fusion(f32[16,256,256]{2,1,0:T(8,128)} %all-gather.4.cloned.1.call-done, f32[16,256,256]{2,1,0:T(8,128)} %gather_fusion.3, pred[16]{0:T(512)(128)(4,1)S(1)} %compare_and_fusion.4), kind=kOutput, calls=%fused_computation.18 | convolution fusion | flops 3222274048 | bytes 12582928 | tf_op jit(solution)/shard_map/kab,kbd->kad/dot_general | solution.py:51
  83.8 4.2 gather_fusion.5
  88.0 95.9 %all-reduce.2.cloned.1.call-done = f32[16,256,256]{2,1,0:T(8,128)} async-done(((f32[16,256,256]{2,1,0:T(8,128)}), f32[16,256,256]{2,1,0:T(8,128)}) %all-reduce.2.cloned.1.call-update) | async-done | bytes 4194320 | tf_op jit(solution)/shard_map/psum | solution.py:98
  183.9 4.6 neg.15
  188.4 4.2 gather_fusion.6
  192.6 6.1 fusion.17
  201.2 4.4 scatter_fusion
  212.8 45.9 %all-gather.6.cloned.1.call-done = f32[16,512,256]{2,1,0:T(8,128)} async-done(((f32[1,512,256]{2,1,0:T(8,128)}), f32[16,512,256]{2,1,0:T(8,128)}) %all-gather.6.cloned.1.call-update) | async-done | bytes 8388624 | tf_op jit(solution)/shard_map/all_gather | solution.py:19
  258.7 8.3 fusion
  269.2 3.1 copy-done.1
  278.3 60.6 %reduce-scatter.3.cloned.1.call-done = f32[1,256,256]{2,1,0:T(8,128)} async-done(((f32[16,256,256]{2,1,0:T(8,128)}), f32[1,256,256]{2,1,0:T(8,128)}) %reduce-scatter.3.cloned.1.call-update) | async-done | bytes 262160 | tf_op jit(solution)/shard_map/reduce_scatter | solution.py:113
  341.4 4.3 all-to-all-start
  352.9 4.6 gather_fusion.9
  357.5 2.9 gather_fusion.10
  360.4 6.7 fusion.22
  369.4 5.3 scatter_fusion.1
  374.7 15.3 %all-to-all-done = f32[8,1,256,256]{3,2,1,0:T(8,128)} async-done(((f32[8,1,256,256]{3,2,1,0:T(8,128)}), f32[8,1,256,256]{3,2,1,0:T(8,128)}, u32[]{:S(2)}, u32[]{:S(2)}) %all-to-all-start) | async-done | bytes 2097184 | tf_op jit(solution)/shard_map/all_to_all | solution.py:25
  391.8 2.8 fusion.37
  394.6 294.3 %all-gather.8.cloned.1.call-done = f32[8,16,256,256]{3,2,1,0:T(8,128)} async-done(((f32[1,16,256,256]{3,2,1,0:T(8,128)}), f32[8,16,256,256]{3,2,1,0:T(8,128)}) %all-gather.8.cloned.1.call-update) | async-done | bytes 33554448 | tf_op jit(solution)/shard_map/all_gather | solution.py:9
  688.9 14.3 %reduce_sum.31 = f32[16,256,256]{2,1,0:T(8,128)} reduce(f32[8,16,256,256]{3,2,1,0:T(8,128)} %all-gather.8.cloned.1.call-done, f32[]{:T(128)} %constant.166.clone.1), dimensions={0}, to_apply=%region_5.9 | reduce | flops 7340032 | bytes 37748740 | tf_op jit(solution)/shard_map/reduce_sum | solution.py:9
  703.2 4.5 neg.16
  707.7 4.2 gather_fusion.11
  711.8 6.7 fusion.27
  721.0 4.4 scatter_fusion.2
  725.4 7.4 pad_maximum_fusion
  732.8 99.5 %reduce-scatter.5.cloned.1.call-done = f32[1,512,256]{2,1,0:T(8,128)} async-done(((f32[16,512,256]{2,1,0:T(8,128)}), f32[1,512,256]{2,1,0:T(8,128)}) %reduce-scatter.5.cloned.1.call-update) | async-done | bytes 524304 | tf_op jit(solution)/shard_map/reduce_scatter | solution.py:34
  833.7 4.1 broadcast_in_dim.125
  837.9 4.9 all-to-all-start.1
  846.6 44.8 %all-to-all-done.1 = f32[8,1,131072]{2,1,0:T(1,128)} async-done(((f32[8,1,131072]{2,1,0:T(1,128)}), f32[8,1,131072]{2,1,0:T(1,128)}, u32[]{:S(2)}, u32[]{:S(2)}) %all-to-all-start.1) | async-done | bytes 4194336 | tf_op jit(solution)/shard_map/all_to_all | solution.py:25
  891.4 5.2 reduce_sum.32
  (96 shorter events, 48.1 us)
Async XLA Ops:
  7.2 62.9 %all-gather.4.cloned.1.call-start = ((), (), s32[]{:S(2)}) async-start(), calls=%async_computation.4 | async-start | bytes 4456448 | tf_op jit(solution)/shard_map/all_gather | solution.py:88
  7.9 176.0 %all-reduce.2.cloned.1.call-start = ((), (), s32[]{:S(2)}) async-start(), calls=%async_computation.5 | async-start | bytes 8388608 | tf_op jit(solution)/shard_map/psum | solution.py:98
  79.7 0.9 copy-start.5
  79.7 1.0 copy-start.8
  79.8 178.9 %all-gather.6.cloned.1.call-start = ((), (), s32[]{:S(2)}) async-start(), calls=%async_computation.7 | async-start | bytes 8912896 | tf_op jit(solution)/shard_map/all_gather | solution.py:19
  81.6 257.4 %reduce-scatter.3.cloned.1.call-start = ((), (), s32[]{:S(2)}) async-start(), calls=%async_computation.6 | async-start | bytes 4456448 | tf_op jit(solution)/shard_map/reduce_scatter | solution.py:113
  201.2 5.0 copy-start
  205.6 483.3 %all-gather.8.cloned.1.call-start = ((), (), s32[]{:S(2)}) async-start(), calls=%async_computation.8 | async-start | bytes 37748736 | tf_op jit(solution)/shard_map/all_gather | solution.py:9
  267.0 5.3 copy-start.1
  274.9 1.9 copy-start.3
  278.3 73.9 %copy-start.9 = (s32[3]{0:T(128)S(1)}, s32[3]{0:T(128)}, u32[]{:S(2)}) copy-start(s32[3]{0:T(128)} %constant.174.clone.1) | copy-start | bytes 40
  341.4 48.6 %all-to-all-start = ((f32[8,1,256,256]{3,2,1,0:T(8,128)}), f32[8,1,256,256]{3,2,1,0:T(8,128)}, u32[]{:S(2)}, u32[]{:S(2)}) async-start(f32[8,1,256,256]{3,2,1,0:T(8,128)} %broadcast_in_dim.110), calls=%async_computation.1 | async-start | bytes 4194304 | tf_op jit(solution)/shard_map/all_to_all | solution.py:25
  345.8 486.6 %reduce-scatter.5.cloned.1.call-start = ((), (), s32[]{:S(2)}) async-start(), calls=%async_computation.9 | async-start | bytes 8912896 | tf_op jit(solution)/shard_map/reduce_scatter | solution.py:34
  369.4 22.3 %copy-start.6 = (f32[1,256,256]{2,1,0:T(8,128)S(1)}, f32[1,256,256]{2,1,0:T(8,128)}, u32[]{:S(2)}) copy-start(f32[1,256,256]{2,1,0:T(8,128)} %param.20) | copy-start | bytes 786436
  391.8 311.4 %copy-start.4 = (f32[1,256,256]{2,1,0:T(8,128)}, f32[1,256,256]{2,1,0:T(8,128)S(1)}, u32[]{:S(2)}) copy-start(f32[1,256,256]{2,1,0:T(8,128)S(1)} %bitcast_subtract_fusion) | copy-start | bytes 786436
  718.5 2.4 copy-start.2
  837.9 4.9 copy-start.7
  837.9 53.6 %all-to-all-start.1 = ((f32[8,1,131072]{2,1,0:T(1,128)}), f32[8,1,131072]{2,1,0:T(1,128)}, u32[]{:S(2)}, u32[]{:S(2)}) async-start(f32[8,1,131072]{2,1,0:T(1,128)} %broadcast_in_dim.125), calls=%async_computation.3 | async-start | bytes 8388608 | tf_op jit(solution)/shard_map/all_to_all | solution.py:25
Sparse Core Ops, SparseCore 0:
  10.4 59.5 all-gather.3
  79.9 103.9 all-reduce.1
  186.9 71.8 all-gather.5
  262.6 76.3 reduce-scatter.2
  340.6 348.3 all-gather.7
  732.9 99.3 reduce-scatter.4
